TPU v7x, 256 devices: a whole 4x4x8 slice. The times are simulated.
256 devices in a mesh: dp: 2 (over core), row: 16 (over x, y), col: 8 (over z).
Axes of the slice: x: 4, y: 4, z: 8, core: 2. Of those that a mesh axis runs over, the one named last changes fastest.
Arguments:
- tokens: bfloat16 [1536, 8192], P('dp', 'row'), may hold values from -6 to 6
- out_grad: bfloat16 [1536, 8192], P('dp', 'row'), may hold values from -6 to 6
- gate_weight: bfloat16 [8192, 14336], P('row', 'col'), may hold values from -0.0625 to 0.0625
- up_weight: bfloat16 [8192, 14336], P('row', 'col'), may hold values from -0.0625 to 0.0625
- down_weight: bfloat16 [14336, 8192], P('col', 'row'), may hold values from -0.046875 to 0.046875
- gate_mask: int32 [64, 112], P('row', 'col'), may hold values from 0 to 1, as said below
- up_mask: int32 [64, 112], P('row', 'col'), may hold values from 0 to 1, as said below
- down_mask: int32 [112, 64], P('col', 'row'), may hold values from 0 to 1, as said below
Outputs:
- output: bfloat16 [1536, 8192], P(('dp', 'col'), 'row')
- token_grad: bfloat16 [1536, 8192], P(('dp', 'col'), 'row')
- gate_grad: bfloat16 [8192, 14336], P('row', 'col')
- up_grad: bfloat16 [8192, 14336], P('row', 'col')
- down_grad: bfloat16 [14336, 8192], P('col', 'row')
Inputs may be any that keep to these rules, and one draw needn't show every extreme that they name: `gate_mask`: one keep flag for each 128 x 128 block of the matrix; the share kept differs from block row to block row. `up_mask`: one keep flag for each 128 x 128 block of the matrix; the share kept differs from block row to block row. `down_mask`: one keep flag for each 128 x 128 block of the matrix; the share kept differs from block column to block column.
All inputs are finite; a program needn't handle non-finite values.
Results may differ from a plain program's by a relative error of at most 0.029.
Values may be sent and summed in bfloat16 or wider, within the bound.
A program may use at most 128 MiB of HBM per device.

v0:
```python
import jax
import jax.numpy as jnp
from jax import lax
from jax.sharding import PartitionSpec as P

BLOCK = 128


def expand(mask_tile):
    return jnp.repeat(jnp.repeat(mask_tile, BLOCK, axis=0), BLOCK, axis=1)


def contract_rows(left_side, right_side):
    return lax.dot_general(
        left_side, right_side, (((0,), (0,)), ((), ())), preferred_element_type=jnp.float32
    )


def contract_cols(left_side, right_side):
    return lax.dot_general(
        left_side, right_side, (((1,), (1,)), ((), ())), preferred_element_type=jnp.float32
    )


def body(tokens, out_grad, gate_weight, up_weight, down_weight, gate_mask, up_mask, down_mask):
    gate_keep = expand(gate_mask)
    up_keep = expand(up_mask)
    down_keep = expand(down_mask)
    gate_eff = gate_weight * gate_keep.astype(jnp.bfloat16)
    up_eff = up_weight * up_keep.astype(jnp.bfloat16)
    down_eff = down_weight * down_keep.astype(jnp.bfloat16)
    gate_part = jnp.dot(tokens, gate_eff, preferred_element_type=jnp.float32)
    up_part = jnp.dot(tokens, up_eff, preferred_element_type=jnp.float32)
    gate_share, up_share = (
        lax.psum_scatter(
            gate_part.astype(jnp.bfloat16), "row", scatter_dimension=0, tiled=True
        ).astype(jnp.float32),
        lax.psum_scatter(
            up_part.astype(jnp.bfloat16), "row", scatter_dimension=0, tiled=True
        ).astype(jnp.float32),
    )
    gate_sig = jax.nn.sigmoid(gate_share)
    silu_gate = gate_share * gate_sig
    hidden_share = (silu_gate * up_share).astype(jnp.bfloat16)
    hidden = lax.all_gather(hidden_share, "row", axis=0, tiled=True)
    output = lax.psum_scatter(
        jnp.dot(hidden, down_eff, preferred_element_type=jnp.float32).astype(jnp.bfloat16),
        "col",
        scatter_dimension=0,
        tiled=True,
    )
    down_local = contract_rows(hidden, out_grad) * down_keep.astype(jnp.float32)
    back_part = contract_cols(out_grad, down_eff)
    back_share = lax.psum_scatter(
        back_part.astype(jnp.bfloat16), "row", scatter_dimension=0, tiled=True
    ).astype(jnp.float32)
    gate_deriv = (back_share * up_share * gate_sig * (1.0 + gate_share * (1.0 - gate_sig))).astype(
        jnp.bfloat16
    )
    up_deriv = (back_share * silu_gate).astype(jnp.bfloat16)
    gate_full, up_full = (
        lax.all_gather(gate_deriv, "row", axis=0, tiled=True),
        lax.all_gather(up_deriv, "row", axis=0, tiled=True),
    )
    token_grad = lax.psum_scatter(
        (contract_cols(gate_full, gate_eff) + contract_cols(up_full, up_eff)).astype(jnp.bfloat16),
        "col",
        scatter_dimension=0,
        tiled=True,
    )
    gate_local = contract_rows(tokens, gate_full) * gate_keep.astype(jnp.float32)
    up_local = contract_rows(tokens, up_full) * up_keep.astype(jnp.float32)
    gate_total, up_total, down_total = (
        lax.psum(gate_local.astype(jnp.bfloat16), "dp").astype(jnp.float32),
        lax.psum(up_local.astype(jnp.bfloat16), "dp").astype(jnp.float32),
        lax.psum(down_local.astype(jnp.bfloat16), "dp").astype(jnp.float32),
    )
    return (
        output,
        token_grad,
        gate_total.astype(jnp.bfloat16),
        up_total.astype(jnp.bfloat16),
        down_total.astype(jnp.bfloat16),
    )


def solution(mesh):
    placed = (
        P("dp", "row"),
        P("dp", "row"),
        P("row", "col"),
        P("row", "col"),
        P("col", "row"),
        P("row", "col"),
        P("row", "col"),
        P("col", "row"),
    )
    return jax.shard_map(
        body,
        mesh=mesh,
        in_specs=placed,
        out_specs=(
            P(("dp", "col"), "row"),
            P(("dp", "col"), "row"),
            P("row", "col"),
            P("row", "col"),
            P("col", "row"),
        ),
        check_vma=False,
    )
```

profile of v0, /device:TPU:2, one launch (start us, length us, event | category | flops | bytes accessed | tf_op | source)
XLA Modules:
  0.0 568.2 jit_solution(9316289985637627538)
XLA Ops:
  8.2 5.1 broadcast_in_dim.35
  13.3 1.2 copy-done.8
  14.5 1.6 fusion.5
  16.2 2.9 copy.59
  19.1 2.8 copy.43
  22.3 1.2 copy-done.4
  23.6 1.6 fusion.3
  25.2 2.9 copy.55
  28.2 2.8 copy.46
  31.4 1.2 copy-done.5
  32.6 1.6 fusion.4
  34.2 2.9 copy.57
  37.2 66.0 %reduce-scatter.20.cloned.1.call-done = bf16[48,1792]{1,0:T(8,128)(2,1)} async-done(((bf16[768,1792]{1,0:T(8,128)(2,1)}), bf16[48,1792]{1,0:T(8,128)(2,1)}) %reduce-scatter.20.cloned.1.call-update) | async-done | bytes 172048 | tf_op jit(solution)/shard_map/reduce_scatter | solution.py:54
  103.2 84.2 %reduce-scatter.16.cloned.1.call-done = bf16[48,1792]{1,0:T(8,128)(2,1)} async-done(((bf16[768,1792]{1,0:T(8,128)(2,1)}), bf16[48,1792]{1,0:T(8,128)(2,1)}) %reduce-scatter.16.cloned.1.call-update) | async-done | bytes 172048 | tf_op jit(solution)/shard_map/reduce_scatter | solution.py:35
  187.5 84.3 %reduce-scatter.18.cloned.1.call-done = bf16[48,1792]{1,0:T(8,128)(2,1)} async-done(((bf16[768,1792]{1,0:T(8,128)(2,1)}), bf16[48,1792]{1,0:T(8,128)(2,1)}) %reduce-scatter.18.cloned.1.call-update) | async-done | bytes 172048 | tf_op jit(solution)/shard_map/reduce_scatter | solution.py:38
  271.7 2.1 fusion.10
  275.7 48.8 %all-gather.6.cloned.1.call-done = bf16[768,1792]{1,0:T(8,128)(2,1)} async-done(((bf16[48,1792]{1,0:T(8,128)(2,1)}), bf16[768,1792]{1,0:T(8,128)(2,1)}) %all-gather.6.cloned.1.call-update) | async-done | bytes 2752528 | tf_op jit(solution)/shard_map/all_gather | solution.py:62
  324.5 4.7 fusion.2
  329.2 48.4 %all-gather.8.cloned.1.call-done = bf16[768,1792]{1,0:T(8,128)(2,1)} async-done(((bf16[48,1792]{1,0:T(8,128)(2,1)}), bf16[768,1792]{1,0:T(8,128)(2,1)}) %all-gather.8.cloned.1.call-update) | async-done | bytes 2752528 | tf_op jit(solution)/shard_map/all_gather | solution.py:63
  377.6 4.7 fusion.1
  382.3 48.4 %all-gather.4.cloned.1.call-done = bf16[768,1792]{1,0:T(8,128)(2,1)} async-done(((bf16[48,1792]{1,0:T(8,128)(2,1)}), bf16[768,1792]{1,0:T(8,128)(2,1)}) %all-gather.4.cloned.1.call-update) | async-done | bytes 2752528 | tf_op jit(solution)/shard_map/all_gather | solution.py:45
  430.8 2.2 broadcast_in_dim.41
  433.0 2.9 fusion
  436.0 5.5 convolution_convert_fusion.3
  441.6 3.2 fusion.18
  444.8 2.5 add_convert_fusion
  447.3 29.8 %all-reduce.3.cloned.1.call-done = (bf16[512,1792]{0,1:T(8,128)(2,1)}, bf16[512,1792]{0,1:T(8,128)(2,1)}, bf16[1792,512]{1,0:T(8,128)(2,1)}) async-done(((bf16[512,1792]{0,1:T(8,128)(2,1)}, bf16[512,1792]{0,1:T(8,128)(2,1)}, bf16[1792,512]{1,0:T(8,128)(2,1)}), (bf16[512,1792]{0,1:T(8,128)(2,1)}, bf16[512,1792]{0,1:T(8,128)(2,1)}, bf16[1792,512]{1,0:T(8,128)(2,1)})) %all-reduce.3.cloned.1.call-update) | async-done | bytes 5505040 | tf_op jit(solution)/shard_map/psum | solution.py:74
  477.1 3.8 copy.53
  480.9 3.9 copy.54
  484.8 35.0 %reduce-scatter.12.cloned.1.call-done = bf16[96,512]{1,0:T(8,128)(2,1)} async-done(((bf16[768,512]{1,0:T(8,128)(2,1)}), bf16[96,512]{1,0:T(8,128)(2,1)}) %reduce-scatter.12.cloned.1.call-update) | async-done | bytes 98320 | tf_op jit(solution)/shard_map/reduce_scatter | solution.py:46
  519.9 40.1 %reduce-scatter.14.cloned.1.call-done = bf16[96,512]{1,0:T(8,128)(2,1)} async-done(((bf16[768,512]{1,0:T(8,128)(2,1)}), bf16[96,512]{1,0:T(8,128)(2,1)}) %reduce-scatter.14.cloned.1.call-update) | async-done | bytes 98320 | tf_op jit(solution)/shard_map/reduce_scatter | solution.py:65
  560.0 1.2 copy.74
  (70 shorter events, 4.4 us)
Async XLA Ops:
  7.2 16.4 %copy-start = (bf16[768,512]{1,0:T(8,128)(2,1)S(1)}, bf16[768,512]{1,0:T(8,128)(2,1)}, u32[]{:S(2)}) copy-start(bf16[768,512]{1,0:T(8,128)(2,1)} %param.8) | copy-start | bytes 2359300
  7.2 96.1 %reduce-scatter.20.cloned.1.call-start = ((), (), s32[]{:S(2)}) async-start(), calls=%async_computation.12 | async-start | bytes 2924544 | tf_op jit(solution)/shard_map/reduce_scatter | solution.py:54
  8.1 6.4 %copy-start.12 = (bf16[1792,512]{1,0:T(8,128)(2,1)S(1)}, bf16[1792,512]{1,0:T(8,128)(2,1)}, u32[]{:S(2)}) copy-start(bf16[1792,512]{1,0:T(8,128)(2,1)} %param.12) | copy-start | bytes 5505028
  8.1 6.4 %copy-start.13 = (bf16[768,512]{1,0:T(8,128)(2,1)S(1)}, bf16[768,512]{1,0:T(8,128)(2,1)}, u32[]{:S(2)}) copy-start(bf16[768,512]{1,0:T(8,128)(2,1)} %param.9) | copy-start | bytes 2359300
  13.3 1.2 copy-start.8
  19.1 2.9 copy-start.9
  19.1 168.4 %reduce-scatter.16.cloned.1.call-start = ((), (), s32[]{:S(2)}) async-start(), calls=%async_computation.10 | async-start | bytes 2924544 | tf_op jit(solution)/shard_map/reduce_scatter | solution.py:35
  22.3 1.2 copy-start.4
  28.1 2.9 copy-start.10
  28.1 243.6 %reduce-scatter.18.cloned.1.call-start = ((), (), s32[]{:S(2)}) async-start(), calls=%async_computation.11 | async-start | bytes 2924544 | tf_op jit(solution)/shard_map/reduce_scatter | solution.py:38
  31.4 1.2 copy-start.5
  37.2 287.3 %all-gather.6.cloned.1.call-start = ((), (), s32[]{:S(2)}) async-start(), calls=%async_computation.7 | async-start | bytes 2924544 | tf_op jit(solution)/shard_map/all_gather | solution.py:62
  273.8 103.8 %all-gather.8.cloned.1.call-start = ((), (), s32[]{:S(2)}) async-start(), calls=%async_computation.8 | async-start | bytes 2924544 | tf_op jit(solution)/shard_map/all_gather | solution.py:63
  274.4 156.3 %all-gather.4.cloned.1.call-start = ((), (), s32[]{:S(2)}) async-start(), calls=%async_computation.5 | async-start | bytes 2924544 | tf_op jit(solution)/shard_map/all_gather | solution.py:45
  275.0 202.1 %all-reduce.3.cloned.1.call-start = ((), (), s32[]{:S(2)}) async-start(), calls=%async_computation.13 | async-start | bytes 11010048 | tf_op jit(solution)/shard_map/psum | solution.py:74
  430.7 2.2 copy-start.11
  430.8 2.2 copy-start.14
  435.9 5.7 copy-start.2
  435.9 83.9 %reduce-scatter.12.cloned.1.call-start = ((), (), s32[]{:S(2)}) async-start(), calls=%async_computation.6 | async-start | bytes 884736 | tf_op jit(solution)/shard_map/reduce_scatter | solution.py:46
  441.5 118.5 %reduce-scatter.14.cloned.1.call-start = ((), (), s32[]{:S(2)}) async-start(), calls=%async_computation.9 | async-start | bytes 884736 | tf_op jit(solution)/shard_map/reduce_scatter | solution.py:65
  441.6 3.3 copy-start.3
  441.6 3.3 copy-start.6
  480.9 79.1 %copy-start.7 = (bf16[1792,512]{1,0:T(8,128)(2,1)S(1)}, bf16[1792,512]{1,0:T(8,128)(2,1)}, u32[]{:S(2)}) copy-start(bf16[1792,512]{1,0:T(8,128)(2,1)} %get-tuple-element.41) | copy-start | bytes 5505028
  560.0 1.7 copy-start.1
Sparse Core Ops, SparseCore 0:
  19.2 84.0 reduce-scatter.19
  106.8 80.5 reduce-scatter.15
  191.1 80.5 reduce-scatter.17
  274.1 50.4 all-gather.5
  326.9 50.6 all-gather.7
  379.9 50.6 all-gather.3
  436.0 41.0 all-reduce.2
  480.2 39.6 reduce-scatter.11
  523.0 36.9 reduce-scatter.13
where the time goes:
time: 569 us; the launch traced here: 568 us
  waiting for transfers between devices  486 us (85%)
  local copies, waits for them, and re-layouts  35.8 us (6%)
  matrix products  28.4 us (5%)
  between operations  14.2 us (2%)
    reduce_scatter x1, waiting for transfers between devices, body(): lax.psum_scatter(up_part.astype(jnp.bfloat16), 'row', scatter_dimension=0...  84.3 us
    reduce_scatter x1, waiting for transfers between devices, body(): lax.psum_scatter(gate_part.astype(jnp.bfloat16), 'row', scatter_dimension...  84.2 us
    reduce_scatter x1, waiting for transfers between devices, body(): lax.psum_scatter(back_part.astype(jnp.bfloat16), 'row', scatter_dimension...  66 us
    all_gather x1, waiting for transfers between devices, body(): lax.all_gather(gate_deriv, 'row', axis=0, tiled=True)  48.8 us
    all_gather x1, waiting for transfers between devices, body(): hidden = lax.all_gather(hidden_share, 'row', axis=0, tiled=True)  48.4 us
    all_gather x1, waiting for transfers between devices, body(): lax.all_gather(up_deriv, 'row', axis=0, tiled=True)  48.4 us
    reduce_scatter x1, waiting for transfers between devices, body(): lax.psum_scatter((contract_cols(gate_full, gate_eff) + contract_cols(up_f...  40.1 us
    reduce_scatter x1, waiting for transfers between devices, body(): lax.psum_scatter(jnp.dot(hidden, down_eff, preferred_element_type=jnp.flo...  35 us
  transfers between devices with their start and end apart: 9, of which 9 were waited for; matrix products, arithmetic and copies ran while one was open for 8% of the time, Pallas kernels for 0%

commit v1 on v0

--- a/solution.py
+++ b/solution.py
@@ -4,6 +4,11 @@
 from jax.sharding import PartitionSpec as P
 
 BLOCK = 128
+
+
+def exchange_gather(shard, mesh_axis, dim):
+    repeated = jnp.stack([shard] * lax.axis_size(mesh_axis))
+    return jnp.concatenate(lax.all_to_all(repeated, mesh_axis, 0, 0), axis=dim)
 
 
 def expand(mask_tile):
@@ -59,7 +64,7 @@
     )
     up_deriv = (back_share * silu_gate).astype(jnp.bfloat16)
     gate_full, up_full = (
-        lax.all_gather(gate_deriv, "row", axis=0, tiled=True),
+        exchange_gather(gate_deriv, "row", 0),
         lax.all_gather(up_deriv, "row", axis=0, tiled=True),
     )
     token_grad = lax.psum_scatter(

time: 569 us -> 538 us (0.946)
  waiting for transfers between devices: 486 us -> 446 us
    all_gather x1 -> x0, waiting for transfers between devices: 48.8 us -> none  [body(): lax.all_gather(gate_deriv, 'row', axis=0, tiled=True)]
    all_to_all x0 -> x1, waiting for transfers between devices: none -> 32.9 us  [exchange_gather(): return jnp.concatenate(lax.all_to_all(repeated, mesh_axis, 0, 0), axis=dim)]
    all_gather x1, waiting for transfers between devices: 48.4 us -> 24.9 us  [body(): lax.all_gather(up_deriv, 'row', axis=0, tiled=True)]
    unnamed x50 -> x48, local copies, waits for them, and re-layouts: 27.8 us -> 29 us
  transfers between devices with their start and end apart: 9 -> 9, of which waited for: 9 -> 9; matrix products, arithmetic and copies ran while one was open for 8% -> 9% of each run, Pallas kernels for 0% -> 0%
where the time goes in v1:
time: 538 us; the launch traced here: 537 us
  waiting for transfers between devices  446 us (83%)
  local copies, waits for them, and re-layouts  39.4 us (7%)
  matrix products  27.1 us (5%)
  between operations  14.4 us (3%)
  starting transfers between devices  6.17 us (1%)
    reduce_scatter x1, waiting for transfers between devices, body(): lax.psum_scatter(up_part.astype(jnp.bfloat16), 'row', scatter_dimension=0...  84.4 us
    reduce_scatter x1, waiting for transfers between devices, body(): lax.psum_scatter(gate_part.astype(jnp.bfloat16), 'row', scatter_dimension...  84.4 us
    reduce_scatter x1, waiting for transfers between devices, body(): lax.psum_scatter(back_part.astype(jnp.bfloat16), 'row', scatter_dimension...  65.5 us
    all_gather x1, waiting for transfers between devices, body(): hidden = lax.all_gather(hidden_share, 'row', axis=0, tiled=True)  48.4 us
    reduce_scatter x1, waiting for transfers between devices, body(): lax.psum_scatter((contract_cols(gate_full, gate_eff) + contract_cols(up_f...  40.1 us
    reduce_scatter x1, waiting for transfers between devices, body(): lax.psum_scatter(jnp.dot(hidden, down_eff, preferred_element_type=jnp.flo...  35 us
    all_to_all x1, waiting for transfers between devices, exchange_gather(): return jnp.concatenate(lax.all_to_all(repeated, mesh_axis, 0, 0), axis=dim)  32.9 us
    psum x1, waiting for transfers between devices, body(): lax.psum(gate_local.astype(jnp.bfloat16), 'dp').astype(jnp.float32)  29.9 us
  transfers between devices with their start and end apart: 9, of which 9 were waited for; matrix products, arithmetic and copies ran while one was open for 9% of the time, Pallas kernels for 0%

profile of v1, /device:TPU:2, one launch (start us, length us, event | category | flops | bytes accessed | tf_op | source)
XLA Modules:
  0.0 537.1 jit_solution(3253094477257127090)
XLA Ops:
  8.2 5.1 broadcast_in_dim.35
  13.3 1.2 copy-done.7
  14.5 1.6 fusion.5
  16.2 2.9 copy.61
  19.1 2.8 copy.45
  23.6 1.6 fusion.3
  25.2 2.9 copy.57
  28.2 2.8 copy.48
  33.2 1.6 fusion.4
  34.8 2.8 copy.59
  37.7 65.5 %reduce-scatter.20.cloned.1.call-done = bf16[48,1792]{1,0:T(8,128)(2,1)} async-done(((bf16[768,1792]{1,0:T(8,128)(2,1)}), bf16[48,1792]{1,0:T(8,128)(2,1)}) %reduce-scatter.20.cloned.1.call-update) | async-done | bytes 172048 | tf_op jit(solution)/shard_map/reduce_scatter | solution.py:59
  103.3 84.4 %reduce-scatter.16.cloned.1.call-done = bf16[48,1792]{1,0:T(8,128)(2,1)} async-done(((bf16[768,1792]{1,0:T(8,128)(2,1)}), bf16[48,1792]{1,0:T(8,128)(2,1)}) %reduce-scatter.16.cloned.1.call-update) | async-done | bytes 172048 | tf_op jit(solution)/shard_map/reduce_scatter | solution.py:40
  187.7 84.4 %reduce-scatter.18.cloned.1.call-done = bf16[48,1792]{1,0:T(8,128)(2,1)} async-done(((bf16[768,1792]{1,0:T(8,128)(2,1)}), bf16[48,1792]{1,0:T(8,128)(2,1)}) %reduce-scatter.18.cloned.1.call-update) | async-done | bytes 172048 | tf_op jit(solution)/shard_map/reduce_scatter | solution.py:43
  272.1 2.1 fusion.10
  274.8 1.7 stack.2
  276.5 5.7 %all-to-all-start = ((bf16[16,48,1792]{2,1,0:T(8,128)(2,1)}), bf16[16,48,1792]{2,1,0:T(8,128)(2,1)S(1)}, u32[]{:S(2)}, u32[]{:S(2)}) async-start(bf16[16,48,1792]{2,1,0:T(8,128)(2,1)} %stack.2), calls=%async_computation.1 | async-start | bytes 5505024 | tf_op jit(solution)/shard_map/all_to_all | solution.py:11
  284.8 32.9 %all-to-all-done = bf16[16,48,1792]{2,1,0:T(8,128)(2,1)S(1)} async-done(((bf16[16,48,1792]{2,1,0:T(8,128)(2,1)}), bf16[16,48,1792]{2,1,0:T(8,128)(2,1)S(1)}, u32[]{:S(2)}, u32[]{:S(2)}) %all-to-all-start) | async-done | bytes 2752544 | tf_op jit(solution)/shard_map/all_to_all | solution.py:11
  317.7 3.6 fusion.2
  321.3 24.9 %all-gather.5.cloned.1.call-done = bf16[768,1792]{1,0:T(8,128)(2,1)} async-done(((bf16[48,1792]{1,0:T(8,128)(2,1)}), bf16[768,1792]{1,0:T(8,128)(2,1)}) %all-gather.5.cloned.1.call-update) | async-done | bytes 2752528 | tf_op jit(solution)/shard_map/all_gather | solution.py:68
  346.3 4.6 fusion.1
  350.9 48.4 %all-gather.3.cloned.1.call-done = bf16[768,1792]{1,0:T(8,128)(2,1)} async-done(((bf16[48,1792]{1,0:T(8,128)(2,1)}), bf16[768,1792]{1,0:T(8,128)(2,1)}) %all-gather.3.cloned.1.call-update) | async-done | bytes 2752528 | tf_op jit(solution)/shard_map/all_gather | solution.py:50
  399.4 2.2 broadcast_in_dim.41
  401.6 2.9 fusion
  404.6 5.4 %convolution_convert_fusion.3 = bf16[768,512]{1,0:T(8,128)(2,1)} fusion(bf16[768,1792]{1,0:T(8,128)(2,1)} %all-gather.3.cloned.1.call-done, bf16[1792,512]{1,0:T(8,128)(2,1)} %param.12, bf16[224,8,4,128]{3,2,1,0:T(4,128)(2,1)} %bitcast.83), kind=kOutput, calls=%fused_computation.16 | convolution fusion | flops 1410596864 | bytes 7208960 | tf_op jit(solution)/shard_map/dot_general | solution.py:52
  410.0 3.2 fusion.18
  413.3 2.5 add_convert_fusion
  415.8 29.9 %all-reduce.3.cloned.1.call-done = (bf16[512,1792]{0,1:T(8,128)(2,1)}, bf16[512,1792]{0,1:T(8,128)(2,1)}, bf16[1792,512]{1,0:T(8,128)(2,1)}) async-done(((bf16[512,1792]{0,1:T(8,128)(2,1)}, bf16[512,1792]{0,1:T(8,128)(2,1)}, bf16[1792,512]{1,0:T(8,128)(2,1)}), (bf16[512,1792]{0,1:T(8,128)(2,1)}, bf16[512,1792]{0,1:T(8,128)(2,1)}, bf16[1792,512]{1,0:T(8,128)(2,1)})) %all-reduce.3.cloned.1.call-update) | async-done | bytes 5505040 | tf_op jit(solution)/shard_map/psum | solution.py:79
  445.7 3.8 copy.55
  449.5 3.9 copy.56
  453.4 35.0 %reduce-scatter.12.cloned.1.call-done = bf16[96,512]{1,0:T(8,128)(2,1)} async-done(((bf16[768,512]{1,0:T(8,128)(2,1)}), bf16[96,512]{1,0:T(8,128)(2,1)}) %reduce-scatter.12.cloned.1.call-update) | async-done | bytes 98320 | tf_op jit(solution)/shard_map/reduce_scatter | solution.py:51
  488.5 40.1 %reduce-scatter.14.cloned.1.call-done = bf16[96,512]{1,0:T(8,128)(2,1)} async-done(((bf16[768,512]{1,0:T(8,128)(2,1)}), bf16[96,512]{1,0:T(8,128)(2,1)}) %reduce-scatter.14.cloned.1.call-update) | async-done | bytes 98320 | tf_op jit(solution)/shard_map/reduce_scatter | solution.py:70
  528.6 1.2 copy.76
  (68 shorter events, 8.7 us)
Async XLA Ops:
  7.2 16.4 %copy-start = (bf16[768,512]{1,0:T(8,128)(2,1)S(1)}, bf16[768,512]{1,0:T(8,128)(2,1)}, u32[]{:S(2)}) copy-start(bf16[768,512]{1,0:T(8,128)(2,1)} %param.8) | copy-start | bytes 2359300
  7.2 96.1 %reduce-scatter.20.cloned.1.call-start = ((), (), s32[]{:S(2)}) async-start(), calls=%async_computation.12 | async-start | bytes 2924544 | tf_op jit(solution)/shard_map/reduce_scatter | solution.py:59
  8.1 6.4 %copy-start.11 = (bf16[1792,512]{1,0:T(8,128)(2,1)S(1)}, bf16[1792,512]{1,0:T(8,128)(2,1)}, u32[]{:S(2)}) copy-start(bf16[1792,512]{1,0:T(8,128)(2,1)} %param.12) | copy-start | bytes 5505028
  8.1 6.4 %copy-start.12 = (bf16[768,512]{1,0:T(8,128)(2,1)S(1)}, bf16[768,512]{1,0:T(8,128)(2,1)}, u32[]{:S(2)}) copy-start(bf16[768,512]{1,0:T(8,128)(2,1)} %param.9) | copy-start | bytes 2359300
  13.3 1.2 copy-start.7
  19.1 2.9 copy-start.8
  19.1 168.6 %reduce-scatter.16.cloned.1.call-start = ((), (), s32[]{:S(2)}) async-start(), calls=%async_computation.10 | async-start | bytes 2924544 | tf_op jit(solution)/shard_map/reduce_scatter | solution.py:40
  22.3 1.2 copy-start.3
  28.1 2.9 copy-start.9
  28.1 244.0 %reduce-scatter.18.cloned.1.call-start = ((), (), s32[]{:S(2)}) async-start(), calls=%async_computation.11 | async-start | bytes 2924544 | tf_op jit(solution)/shard_map/reduce_scatter | solution.py:43
  31.9 1.2 copy-start.4
  37.7 308.6 %all-gather.5.cloned.1.call-start = ((), (), s32[]{:S(2)}) async-start(), calls=%async_computation.8 | async-start | bytes 2924544 | tf_op jit(solution)/shard_map/all_gather | solution.py:68
  274.2 125.2 %all-gather.3.cloned.1.call-start = ((), (), s32[]{:S(2)}) async-start(), calls=%async_computation.6 | async-start | bytes 2924544 | tf_op jit(solution)/shard_map/all_gather | solution.py:50
  276.5 41.2 %all-to-all-start = ((bf16[16,48,1792]{2,1,0:T(8,128)(2,1)}), bf16[16,48,1792]{2,1,0:T(8,128)(2,1)S(1)}, u32[]{:S(2)}, u32[]{:S(2)}) async-start(bf16[16,48,1792]{2,1,0:T(8,128)(2,1)} %stack.2), calls=%async_computation.1 | async-start | bytes 5505024 | tf_op jit(solution)/shard_map/all_to_all | solution.py:11
  282.2 163.5 %all-reduce.3.cloned.1.call-start = ((), (), s32[]{:S(2)}) async-start(), calls=%async_computation.13 | async-start | bytes 11010048 | tf_op jit(solution)/shard_map/psum | solution.py:79
  399.4 2.2 copy-start.10
  399.4 2.2 copy-start.13
  404.5 84.0 %reduce-scatter.12.cloned.1.call-start = ((), (), s32[]{:S(2)}) async-start(), calls=%async_computation.7 | async-start | bytes 884736 | tf_op jit(solution)/shard_map/reduce_scatter | solution.py:51
  410.0 118.6 %reduce-scatter.14.cloned.1.call-start = ((), (), s32[]{:S(2)}) async-start(), calls=%async_computation.9 | async-start | bytes 884736 | tf_op jit(solution)/shard_map/reduce_scatter | solution.py:70
  410.0 3.3 copy-start.2
  410.0 3.3 copy-start.5
  449.5 79.1 %copy-start.6 = (bf16[1792,512]{1,0:T(8,128)(2,1)S(1)}, bf16[1792,512]{1,0:T(8,128)(2,1)}, u32[]{:S(2)}) copy-start(bf16[1792,512]{1,0:T(8,128)(2,1)} %get-tuple-element.41) | copy-start | bytes 5505028
  528.6 1.7 copy-start.1
Sparse Core Ops, SparseCore 0:
  19.2 84.0 reduce-scatter.19
  106.9 80.7 reduce-scatter.15
  191.3 80.7 reduce-scatter.17
  274.4 71.7 all-gather.4
  348.6 50.6 all-gather.2
  404.6 41.0 all-reduce.2
  448.8 39.6 reduce-scatter.11
  491.6 36.9 reduce-scatter.13
